TPU v7x, 128 devices: a whole 4x4x4 slice. The times are simulated.
128 devices in a mesh: src: 8 (over z_hi, y), obs: 16 (over x, z_lo, core).
Axes of the slice: x: 4, y: 4, z: 4 (z_hi: 2, z_lo: 2; z = z_hi * 2 + z_lo), core: 2. Of those that a mesh axis runs over, the one named last changes fastest.
Arguments:
- tiles: bfloat16 [8, 16, 512, 128, 128], P('src', 'obs'), may hold values from -0.25 to 0.25
- tile_index: int32 [8, 16, 3, 512], P('src', 'obs'), may hold values from 0 to 1023, as said below
- tile_count: int32 [8, 16], P('src', 'obs'), may hold values from 64 to 512, as said below
- history: bfloat16 [16, 4, 1048576], P(None, None, ('src', 'obs')), may hold values from -6 to 6
- incident: float32 [2, 4, 1048576], P(None, None, ('src', 'obs')), may hold values from -6 to 6
- near_inverse: bfloat16 [8192, 128, 128], P(('src', 'obs')), may hold values from -0.5 to 0.5
Outputs:
- densities: bfloat16 [2, 4, 1048576], P(None, None, ('src', 'obs'))
Inputs may be any that keep to these rules, and one draw needn't show every extreme that they name: `tile_index`: row 0 is an observer block among the 512 of a device, row 1 a source block among its 1024, row 2 a delay slot below 16; slots at or past the device's count are padding; a tile may repeat. `tile_count`: live tile slots of each device, the first ones of its list.
All inputs are finite; a program needn't handle non-finite values.
Results may differ from a plain program's by a relative error of at most 0.005.
Values may be sent and summed in bfloat16 or wider, within the bound.
A program may use at most 128 MiB of HBM per device.

v0:
```python
import jax
import jax.numpy as jnp
from jax import lax
from jax.sharding import PartitionSpec as P


def on_device(tiles, tile_index, tile_count, history, incident, near_inverse):
    tile_rows = tiles.reshape(tiles.shape[2], tiles.shape[3], tiles.shape[4])
    index_rows = tile_index.reshape(3, tile_index.shape[3])
    live_count = tile_count.reshape(())
    blocks_own = near_inverse.shape[0]
    tile_width = near_inverse.shape[1]
    coefficients = history.shape[1]
    slot_count = history.shape[0]
    observer_owned = blocks_own * lax.axis_size("src")
    total_tiles = tile_rows.shape[0]
    group_size = min(64, total_tiles)
    loop_turns = total_tiles // group_size

    def accumulate(chooser):

        def one_group(turn_index, partial_value):
            start = turn_index * group_size
            tile_part = lax.dynamic_slice_in_dim(tile_rows, start, group_size, 0)
            index_part = lax.dynamic_slice_in_dim(index_rows, start, group_size, 1)
            operand = chooser(index_part, start)
            products = jnp.einsum(
                "gck,gki->cgi", operand, tile_part, preferred_element_type=jnp.float32
            )
            alive_mask = start + jnp.arange(group_size, dtype=jnp.int32) < live_count
            products = jnp.where(alive_mask[None, :, None], products, 0.0)
            return partial_value.at[:, index_part[0]].add(products)

        initial = jnp.zeros((coefficients, observer_owned, tile_width), jnp.float32)
        return lax.fori_loop(0, loop_turns, one_group, initial)

    def settle(partial_value, drive):
        summed = lax.psum(partial_value, "src")
        own_share = lax.dynamic_slice_in_dim(
            summed, lax.axis_index("src") * blocks_own, blocks_own, 1
        )
        right_side = (drive - own_share.reshape(coefficients, blocks_own * tile_width)).astype(
            jnp.bfloat16
        )
        right_side = right_side.reshape(coefficients, blocks_own, tile_width)
        solved = jnp.einsum(
            "cbk,bki->cbi", right_side, near_inverse, preferred_element_type=jnp.float32
        )
        return solved.reshape(coefficients, blocks_own * tile_width).astype(jnp.bfloat16)

    gathered = lax.all_gather(history, "obs", axis=2, tiled=True)
    history_src = gathered.reshape(slot_count, coefficients, -1, tile_width)

    def chooser_first(index_part, start):
        return history_src[index_part[2], :, index_part[1]]

    first_new = settle(accumulate(chooser_first), incident[0])
    newest_src = lax.all_gather(first_new, "obs", axis=1, tiled=True).reshape(
        coefficients, -1, tile_width
    )

    def chooser_second(index_part, start):
        source = index_part[1]
        delay_slot = index_part[2]
        older = history_src[jnp.maximum(delay_slot - 1, 0), :, source]
        newer = jnp.swapaxes(newest_src[:, source], 0, 1)
        return jnp.where((delay_slot == 0)[:, None, None], newer, older)

    second_new = settle(accumulate(chooser_second), incident[1])
    return jnp.stack([first_new, second_new])


def solution(mesh):
    in_specs = (
        P("src", "obs", None, None, None),
        P("src", "obs", None, None),
        P("src", "obs"),
        P(None, None, ("src", "obs")),
        P(None, None, ("src", "obs")),
        P(("src", "obs"), None, None),
    )
    out_specs = P(None, None, ("src", "obs"))
    return jax.shard_map(
        on_device, mesh=mesh, in_specs=in_specs, out_specs=out_specs, check_vma=False
    )
```

profile of v0, /device:TPU:0, one launch (start us, length us, event | category | flops | bytes accessed | tf_op | source)
XLA Modules:
  0.0 536.3 jit_solution(3474233912254696265)
XLA Ops:
  8.0 95.1 %all-gather.3.cloned.1.call-done = bf16[16,4,131072]{2,1,0:T(4,128)(2,1)} async-done(((bf16[16,4,8192]{2,1,0:T(4,128)(2,1)}), bf16[16,4,131072]{2,1,0:T(4,128)(2,1)}) %all-gather.3.cloned.1.call-update) | async-done | bytes 16777232 | tf_op jit(solution)/shard_map/all_gather | solution.py:51
  103.3 98.3 %while.28 = (s32[]{:T(128)}, f32[4,512,128]{2,0,1:T(4,128)S(1)}, s32[3,512]{1,0:T(4,128)S(1)}, s32[]{:T(128)}, bf16[512,128,128]{2,1,0:T(8,128)(2,1)}, /*index=5...) while((s32[]{:T(128)}, f32[4,512,128]{2,0,1:T(4,128)S(1)}, ...), condition=%wide.region_2.3_spmd, body=%wide.region_0.2_spmd.sunk | while | flops 8455174 | bytes 2821923 | solution.py:35
  104.0 6.5 %gather_fusion = bf16[64,4,128]{2,1,0:T(4,128)(2,1)S(1)} fusion(bf16[16,4,1024,128]{3,1,2,0:T(4,128)(2,1)} %get-tuple-element.438, s32[64]{0:T(128)S(1)} %get-tuple-element.402), kind=kCustom, calls=%fused_computation.clone.1 | custom fusion | bytes 131584 | tf_op jit(solution)/shard_map/while/body/eval_jaxpr/gather | solution.py:55
  110.6 2.2 fusion.51
  112.8 2.7 scatter_fusion
  116.3 6.5 %gather_fusion = bf16[64,4,128]{2,1,0:T(4,128)(2,1)S(1)} fusion(bf16[16,4,1024,128]{3,1,2,0:T(4,128)(2,1)} %get-tuple-element.438, s32[64]{0:T(128)S(1)} %get-tuple-element.402), kind=kCustom, calls=%fused_computation.clone.1 | custom fusion | bytes 131584 | tf_op jit(solution)/shard_map/while/body/eval_jaxpr/gather | solution.py:55
  122.8 2.2 fusion.51
  125.1 2.7 scatter_fusion
  128.6 6.5 %gather_fusion = bf16[64,4,128]{2,1,0:T(4,128)(2,1)S(1)} fusion(bf16[16,4,1024,128]{3,1,2,0:T(4,128)(2,1)} %get-tuple-element.438, s32[64]{0:T(128)S(1)} %get-tuple-element.402), kind=kCustom, calls=%fused_computation.clone.1 | custom fusion | bytes 131584 | tf_op jit(solution)/shard_map/while/body/eval_jaxpr/gather | solution.py:55
  135.1 2.2 fusion.51
  137.4 2.7 scatter_fusion
  140.9 6.5 %gather_fusion = bf16[64,4,128]{2,1,0:T(4,128)(2,1)S(1)} fusion(bf16[16,4,1024,128]{3,1,2,0:T(4,128)(2,1)} %get-tuple-element.438, s32[64]{0:T(128)S(1)} %get-tuple-element.402), kind=kCustom, calls=%fused_computation.clone.1 | custom fusion | bytes 131584 | tf_op jit(solution)/shard_map/while/body/eval_jaxpr/gather | solution.py:55
  147.4 2.2 fusion.51
  149.7 2.7 scatter_fusion
  153.2 6.5 %gather_fusion = bf16[64,4,128]{2,1,0:T(4,128)(2,1)S(1)} fusion(bf16[16,4,1024,128]{3,1,2,0:T(4,128)(2,1)} %get-tuple-element.438, s32[64]{0:T(128)S(1)} %get-tuple-element.402), kind=kCustom, calls=%fused_computation.clone.1 | custom fusion | bytes 131584 | tf_op jit(solution)/shard_map/while/body/eval_jaxpr/gather | solution.py:55
  159.7 2.2 fusion.51
  162.0 2.7 scatter_fusion
  165.5 6.5 %gather_fusion = bf16[64,4,128]{2,1,0:T(4,128)(2,1)S(1)} fusion(bf16[16,4,1024,128]{3,1,2,0:T(4,128)(2,1)} %get-tuple-element.438, s32[64]{0:T(128)S(1)} %get-tuple-element.402), kind=kCustom, calls=%fused_computation.clone.1 | custom fusion | bytes 131584 | tf_op jit(solution)/shard_map/while/body/eval_jaxpr/gather | solution.py:55
  172.0 2.2 fusion.51
  174.3 2.7 scatter_fusion
  177.8 6.5 %gather_fusion = bf16[64,4,128]{2,1,0:T(4,128)(2,1)S(1)} fusion(bf16[16,4,1024,128]{3,1,2,0:T(4,128)(2,1)} %get-tuple-element.438, s32[64]{0:T(128)S(1)} %get-tuple-element.402), kind=kCustom, calls=%fused_computation.clone.1 | custom fusion | bytes 131584 | tf_op jit(solution)/shard_map/while/body/eval_jaxpr/gather | solution.py:55
  184.3 2.2 fusion.51
  186.6 2.7 scatter_fusion
  190.1 6.5 %gather_fusion = bf16[64,4,128]{2,1,0:T(4,128)(2,1)S(1)} fusion(bf16[16,4,1024,128]{3,1,2,0:T(4,128)(2,1)} %get-tuple-element.438, s32[64]{0:T(128)S(1)} %get-tuple-element.402), kind=kCustom, calls=%fused_computation.clone.1 | custom fusion | bytes 131584 | tf_op jit(solution)/shard_map/while/body/eval_jaxpr/gather | solution.py:55
  196.6 2.2 fusion.51
  198.8 2.7 scatter_fusion
  202.7 88.8 %all-reduce.3.cloned.1.call-done = f32[4,512,128]{2,0,1:T(4,128)} async-done(((f32[4,512,128]{2,0,1:T(4,128)}), f32[4,512,128]{2,0,1:T(4,128)}) %all-reduce.3.cloned.1.call-update) | async-done | bytes 1048592 | tf_op jit(solution)/shard_map/psum | solution.py:38
  291.6 2.3 convolution_convert_fusion.1
  293.9 30.2 %all-gather.5.cloned.1.call-done = bf16[4,131072]{1,0:T(4,128)(2,1)} async-done(((bf16[4,8192]{1,0:T(4,128)(2,1)}), bf16[4,131072]{1,0:T(4,128)(2,1)}) %all-gather.5.cloned.1.call-update) | async-done | bytes 1048592 | tf_op jit(solution)/shard_map/all_gather | solution.py:58
  324.2 114.0 %while.29 = (s32[]{:T(128)}, f32[4,512,128]{2,0,1:T(4,128)S(1)}, s32[3,512]{1,0:T(4,128)S(1)}, s32[]{:T(128)}, bf16[512,128,128]{2,1,0:T(8,128)(2,1)}, /*index=5...) while((s32[]{:T(128)}, f32[4,512,128]{2,0,1:T(4,128)S(1)}, ...), condition=%wide.region_6.7_spmd, body=%wide.region_4.6_spmd.sunk | while | flops 8488966 | bytes 3023787 | solution.py:35
  325.0 1.9 gather_fusion.1
  326.9 6.5 %gather_fusion.2 = bf16[64,4,128]{2,1,0:T(4,128)(2,1)S(1)} fusion(bf16[16,4,1024,128]{3,1,2,0:T(4,128)(2,1)} %get-tuple-element.471, s32[64]{0:T(128)S(1)} %get-tuple-element.412), kind=kCustom, calls=%fused_computation.2.clone.1 | custom fusion | bytes 131584 | tf_op jit(solution)/shard_map/while/body/eval_jaxpr/gather | solution.py:65
  333.4 2.3 fusion.55
  335.7 2.7 scatter_fusion.1
  339.3 1.9 gather_fusion.1
  341.1 6.5 %gather_fusion.2 = bf16[64,4,128]{2,1,0:T(4,128)(2,1)S(1)} fusion(bf16[16,4,1024,128]{3,1,2,0:T(4,128)(2,1)} %get-tuple-element.471, s32[64]{0:T(128)S(1)} %get-tuple-element.412), kind=kCustom, calls=%fused_computation.2.clone.1 | custom fusion | bytes 131584 | tf_op jit(solution)/shard_map/while/body/eval_jaxpr/gather | solution.py:65
  347.7 2.3 fusion.55
  350.0 2.7 scatter_fusion.1
  353.5 1.9 gather_fusion.1
  355.4 6.5 %gather_fusion.2 = bf16[64,4,128]{2,1,0:T(4,128)(2,1)S(1)} fusion(bf16[16,4,1024,128]{3,1,2,0:T(4,128)(2,1)} %get-tuple-element.471, s32[64]{0:T(128)S(1)} %get-tuple-element.412), kind=kCustom, calls=%fused_computation.2.clone.1 | custom fusion | bytes 131584 | tf_op jit(solution)/shard_map/while/body/eval_jaxpr/gather | solution.py:65
  361.9 2.3 fusion.55
  364.2 2.7 scatter_fusion.1
  367.8 1.9 gather_fusion.1
  369.7 6.5 %gather_fusion.2 = bf16[64,4,128]{2,1,0:T(4,128)(2,1)S(1)} fusion(bf16[16,4,1024,128]{3,1,2,0:T(4,128)(2,1)} %get-tuple-element.471, s32[64]{0:T(128)S(1)} %get-tuple-element.412), kind=kCustom, calls=%fused_computation.2.clone.1 | custom fusion | bytes 131584 | tf_op jit(solution)/shard_map/while/body/eval_jaxpr/gather | solution.py:65
  376.2 2.3 fusion.55
  378.5 2.7 scatter_fusion.1
  382.0 1.9 gather_fusion.1
  383.9 6.5 %gather_fusion.2 = bf16[64,4,128]{2,1,0:T(4,128)(2,1)S(1)} fusion(bf16[16,4,1024,128]{3,1,2,0:T(4,128)(2,1)} %get-tuple-element.471, s32[64]{0:T(128)S(1)} %get-tuple-element.412), kind=kCustom, calls=%fused_computation.2.clone.1 | custom fusion | bytes 131584 | tf_op jit(solution)/shard_map/while/body/eval_jaxpr/gather | solution.py:65
  390.4 2.3 fusion.55
  392.7 2.7 scatter_fusion.1
  396.3 1.9 gather_fusion.1
  398.2 6.5 %gather_fusion.2 = bf16[64,4,128]{2,1,0:T(4,128)(2,1)S(1)} fusion(bf16[16,4,1024,128]{3,1,2,0:T(4,128)(2,1)} %get-tuple-element.471, s32[64]{0:T(128)S(1)} %get-tuple-element.412), kind=kCustom, calls=%fused_computation.2.clone.1 | custom fusion | bytes 131584 | tf_op jit(solution)/shard_map/while/body/eval_jaxpr/gather | solution.py:65
  404.7 2.3 fusion.55
  407.0 2.7 scatter_fusion.1
  410.5 1.9 gather_fusion.1
  412.4 6.5 %gather_fusion.2 = bf16[64,4,128]{2,1,0:T(4,128)(2,1)S(1)} fusion(bf16[16,4,1024,128]{3,1,2,0:T(4,128)(2,1)} %get-tuple-element.471, s32[64]{0:T(128)S(1)} %get-tuple-element.412), kind=kCustom, calls=%fused_computation.2.clone.1 | custom fusion | bytes 131584 | tf_op jit(solution)/shard_map/while/body/eval_jaxpr/gather | solution.py:65
  418.9 2.3 fusion.55
  421.2 2.7 scatter_fusion.1
  424.8 1.9 gather_fusion.1
  426.7 6.5 %gather_fusion.2 = bf16[64,4,128]{2,1,0:T(4,128)(2,1)S(1)} fusion(bf16[16,4,1024,128]{3,1,2,0:T(4,128)(2,1)} %get-tuple-element.471, s32[64]{0:T(128)S(1)} %get-tuple-element.412), kind=kCustom, calls=%fused_computation.2.clone.1 | custom fusion | bytes 131584 | tf_op jit(solution)/shard_map/while/body/eval_jaxpr/gather | solution.py:65
  433.2 2.3 fusion.55
  435.5 2.7 scatter_fusion.1
  439.3 88.1 %all-reduce.5.cloned.1.call-done = f32[4,512,128]{2,0,1:T(4,128)} async-done(((f32[4,512,128]{2,0,1:T(4,128)}), f32[4,512,128]{2,0,1:T(4,128)}) %all-reduce.5.cloned.1.call-update) | async-done | bytes 1048592 | tf_op jit(solution)/shard_map/psum | solution.py:38
  527.4 1.6 fusion.30
  (84 shorter events, 16.7 us)
Async XLA Ops:
  6.5 285.0 %copy-start = (bf16[64,128,128]{2,1,0:T(8,128)(2,1)S(1)}, bf16[64,128,128]{2,1,0:T(8,128)(2,1)}, u32[]{:S(2)}) copy-start(bf16[64,128,128]{2,1,0:T(8,128)(2,1)} %param.15) | copy-start | bytes 6291460
  6.5 96.6 %all-gather.3.cloned.1.call-start = ((), (), s32[]{:S(2)}) async-start(), calls=%async_computation | async-start | bytes 17825792 | tf_op jit(solution)/shard_map/all_gather | solution.py:51
  7.3 284.3 %all-reduce.3.cloned.1.call-start = ((), (), s32[]{:S(2)}) async-start(), calls=%async_computation.1 | async-start | bytes 2097152 | tf_op jit(solution)/shard_map/psum | solution.py:38
  201.6 1.0 copy-start.2
  202.7 121.4 %all-gather.5.cloned.1.call-start = ((), (), s32[]{:S(2)}) async-start(), calls=%async_computation.2 | async-start | bytes 1114112 | tf_op jit(solution)/shard_map/all_gather | solution.py:58
  293.8 233.6 %all-reduce.5.cloned.1.call-start = ((), (), s32[]{:S(2)}) async-start(), calls=%async_computation.3 | async-start | bytes 2097152 | tf_op jit(solution)/shard_map/psum | solution.py:38
  438.2 1.0 copy-start.1
  438.3 90.8 %copy-start.3 = (bf16[64,4,128]{2,1,0:T(4,128)(2,1)S(1)}, bf16[64,4,128]{2,1,0:T(4,128)(2,1)}, u32[]{:S(2)}) copy-start(bf16[64,4,128]{2,1,0:T(4,128)(2,1)} %convolution_convert_fusion.1) | copy-start | bytes 196612
Sparse Core Ops, SparseCore 0:
  9.0 94.0 all-gather.2
  202.8 88.7 all-reduce.2
  294.0 30.0 all-gather.4
  439.4 87.9 all-reduce.4
where the time goes:
time: 538 us; the launch traced here: 536 us
  waiting for transfers between devices  303 us (56%)
  local copies, waits for them, and re-layouts  124 us (23%)
  other arithmetic  55.4 us (10%)
  matrix products  40.1 us (7%)
  between operations  13.2 us (2%)
    psum x2, waiting for transfers between devices, settle(): summed = lax.psum(partial_value, 'src')  177 us
    all_gather x1, waiting for transfers between devices, on_device(): gathered = lax.all_gather(history, 'obs', axis=2, tiled=True)  95.1 us
    gather x8, local copies, waits for them, and re-layouts, chooser_second(): older = history_src[jnp.maximum(delay_slot - 1, 0), :, source]  52.3 us
    gather x8, local copies, waits for them, and re-layouts, chooser_first(): return history_src[index_part[2], :, index_part[1]]  52.2 us
    scatter-add x16, other arithmetic, one_group(): return partial_value.at[:, index_part[0]].add(products)  43.9 us
    dot_general x16, matrix products, one_group(): jnp.einsum('gck,gki->cgi', operand, tile_part, preferred_element_type=jnp...  36.3 us
    all_gather x1, waiting for transfers between devices, on_device(): lax.all_gather(first_new, 'obs', axis=1, tiled=True)  30.2 us
    gather x8, local copies, waits for them, and re-layouts, chooser_second(): newer = jnp.swapaxes(newest_src[:, source], 0, 1)  15 us
  transfers between devices with their start and end apart: 4, of which 4 were waited for; matrix products, arithmetic and copies ran while one was open for 0% of the time, Pallas kernels for 0%

commit v1 on v0

--- a/solution.py
+++ b/solution.py
@@ -35,7 +35,7 @@
         return lax.fori_loop(0, loop_turns, one_group, initial)
 
     def settle(partial_value, drive):
-        summed = lax.psum(partial_value, "src")
+        summed = jnp.sum(lax.all_gather(partial_value, "src"), axis=0)
         own_share = lax.dynamic_slice_in_dim(
             summed, lax.axis_index("src") * blocks_own, blocks_own, 1
         )

time: 538 us -> 585 us (1.087)
  waiting for transfers between devices: 303 us -> 343 us
  other arithmetic: 55.4 us -> 63.2 us
    all_gather x0 -> x2, waiting for transfers between devices: none -> 217 us  [settle(): summed = jnp.sum(lax.all_gather(partial_value, 'src'), axis=0)]
    psum x2 -> x0, waiting for transfers between devices: 177 us -> none  [settle(): summed = lax.psum(partial_value, 'src')]
    reduce_sum x0 -> x2, other arithmetic: none -> 7.82 us  [settle(): summed = jnp.sum(lax.all_gather(partial_value, 'src'), axis=0)]
where the time goes in v1:
time: 585 us; the launch traced here: 583 us
  waiting for transfers between devices  343 us (59%)
  local copies, waits for them, and re-layouts  125 us (21%)
  other arithmetic  63.2 us (11%)
  matrix products  38.3 us (7%)
  between operations  13.2 us (2%)
    all_gather x2, waiting for transfers between devices, settle(): summed = jnp.sum(lax.all_gather(partial_value, 'src'), axis=0)  217 us
    all_gather x1, waiting for transfers between devices, on_device(): gathered = lax.all_gather(history, 'obs', axis=2, tiled=True)  95.1 us
    gather x8, local copies, waits for them, and re-layouts, chooser_second(): older = history_src[jnp.maximum(delay_slot - 1, 0), :, source]  52.3 us
    gather x8, local copies, waits for them, and re-layouts, chooser_first(): return history_src[index_part[2], :, index_part[1]]  52.2 us
    scatter-add x16, other arithmetic, one_group(): return partial_value.at[:, index_part[0]].add(products)  43.9 us
    dot_general x16, matrix products, one_group(): jnp.einsum('gck,gki->cgi', operand, tile_part, preferred_element_type=jnp...  36.4 us
    all_gather x1, waiting for transfers between devices, on_device(): lax.all_gather(first_new, 'obs', axis=1, tiled=True)  29.9 us
    gather x8, local copies, waits for them, and re-layouts, chooser_second(): newer = jnp.swapaxes(newest_src[:, source], 0, 1)  15 us
  transfers between devices with their start and end apart: 4, of which 4 were waited for; matrix products, arithmetic and copies ran while one was open for 0% of the time, Pallas kernels for 0%

profile of v1, /device:TPU:0, one launch (start us, length us, event | category | flops | bytes accessed | tf_op | source)
XLA Modules:
  0.0 583.2 jit_solution(15191931974205112584)
XLA Ops:
  8.0 95.1 %all-gather.7.cloned.1.call-done = bf16[16,4,131072]{2,1,0:T(4,128)(2,1)} async-done(((bf16[16,4,8192]{2,1,0:T(4,128)(2,1)}), bf16[16,4,131072]{2,1,0:T(4,128)(2,1)}) %all-gather.7.cloned.1.call-update) | async-done | bytes 16777232 | tf_op jit(solution)/shard_map/all_gather | solution.py:51
  103.3 98.4 %while.28 = (s32[]{:T(128)}, f32[4,512,128]{2,0,1:T(4,128)S(1)}, s32[3,512]{1,0:T(4,128)S(1)}, s32[]{:T(128)}, bf16[512,128,128]{2,1,0:T(8,128)(2,1)}, /*index=5...) while((s32[]{:T(128)}, f32[4,512,128]{2,0,1:T(4,128)S(1)}, ...), condition=%wide.region_2.3_spmd, body=%wide.region_0.2_spmd.sunk | while | flops 8455174 | bytes 2821923 | solution.py:35
  103.4 6.5 %gather_fusion = bf16[64,4,128]{2,1,0:T(4,128)(2,1)S(1)} fusion(bf16[16,4,1024,128]{3,1,2,0:T(4,128)(2,1)} %get-tuple-element.440, s32[64]{0:T(128)S(1)} %get-tuple-element.404), kind=kCustom, calls=%fused_computation.clone.1 | custom fusion | bytes 131584 | tf_op jit(solution)/shard_map/while/body/eval_jaxpr/gather | solution.py:55
  110.6 2.2 fusion.49
  112.8 2.7 scatter_fusion
  115.7 6.5 %gather_fusion = bf16[64,4,128]{2,1,0:T(4,128)(2,1)S(1)} fusion(bf16[16,4,1024,128]{3,1,2,0:T(4,128)(2,1)} %get-tuple-element.440, s32[64]{0:T(128)S(1)} %get-tuple-element.404), kind=kCustom, calls=%fused_computation.clone.1 | custom fusion | bytes 131584 | tf_op jit(solution)/shard_map/while/body/eval_jaxpr/gather | solution.py:55
  122.8 2.2 fusion.49
  125.1 2.7 scatter_fusion
  128.0 6.5 %gather_fusion = bf16[64,4,128]{2,1,0:T(4,128)(2,1)S(1)} fusion(bf16[16,4,1024,128]{3,1,2,0:T(4,128)(2,1)} %get-tuple-element.440, s32[64]{0:T(128)S(1)} %get-tuple-element.404), kind=kCustom, calls=%fused_computation.clone.1 | custom fusion | bytes 131584 | tf_op jit(solution)/shard_map/while/body/eval_jaxpr/gather | solution.py:55
  135.1 2.2 fusion.49
  137.4 2.7 scatter_fusion
  140.3 6.5 %gather_fusion = bf16[64,4,128]{2,1,0:T(4,128)(2,1)S(1)} fusion(bf16[16,4,1024,128]{3,1,2,0:T(4,128)(2,1)} %get-tuple-element.440, s32[64]{0:T(128)S(1)} %get-tuple-element.404), kind=kCustom, calls=%fused_computation.clone.1 | custom fusion | bytes 131584 | tf_op jit(solution)/shard_map/while/body/eval_jaxpr/gather | solution.py:55
  147.4 2.2 fusion.49
  149.7 2.7 scatter_fusion
  152.5 6.5 %gather_fusion = bf16[64,4,128]{2,1,0:T(4,128)(2,1)S(1)} fusion(bf16[16,4,1024,128]{3,1,2,0:T(4,128)(2,1)} %get-tuple-element.440, s32[64]{0:T(128)S(1)} %get-tuple-element.404), kind=kCustom, calls=%fused_computation.clone.1 | custom fusion | bytes 131584 | tf_op jit(solution)/shard_map/while/body/eval_jaxpr/gather | solution.py:55
  159.7 2.2 fusion.49
  162.0 2.7 scatter_fusion
  164.8 6.5 %gather_fusion = bf16[64,4,128]{2,1,0:T(4,128)(2,1)S(1)} fusion(bf16[16,4,1024,128]{3,1,2,0:T(4,128)(2,1)} %get-tuple-element.440, s32[64]{0:T(128)S(1)} %get-tuple-element.404), kind=kCustom, calls=%fused_computation.clone.1 | custom fusion | bytes 131584 | tf_op jit(solution)/shard_map/while/body/eval_jaxpr/gather | solution.py:55
  172.0 2.2 fusion.49
  174.3 2.7 scatter_fusion
  177.1 6.5 %gather_fusion = bf16[64,4,128]{2,1,0:T(4,128)(2,1)S(1)} fusion(bf16[16,4,1024,128]{3,1,2,0:T(4,128)(2,1)} %get-tuple-element.440, s32[64]{0:T(128)S(1)} %get-tuple-element.404), kind=kCustom, calls=%fused_computation.clone.1 | custom fusion | bytes 131584 | tf_op jit(solution)/shard_map/while/body/eval_jaxpr/gather | solution.py:55
  184.3 2.2 fusion.49
  186.6 2.7 scatter_fusion
  189.4 6.5 %gather_fusion = bf16[64,4,128]{2,1,0:T(4,128)(2,1)S(1)} fusion(bf16[16,4,1024,128]{3,1,2,0:T(4,128)(2,1)} %get-tuple-element.440, s32[64]{0:T(128)S(1)} %get-tuple-element.404), kind=kCustom, calls=%fused_computation.clone.1 | custom fusion | bytes 131584 | tf_op jit(solution)/shard_map/while/body/eval_jaxpr/gather | solution.py:55
  196.6 2.2 fusion.49
  198.9 2.7 scatter_fusion
  203.8 108.3 %all-gather.11.cloned.1.call-done = f32[32,512,128]{2,1,0:T(8,128)} async-done(((f32[4,512,128]{2,1,0:T(8,128)}), f32[32,512,128]{2,1,0:T(8,128)}) %all-gather.11.cloned.1.call-update) | async-done | bytes 8388624 | tf_op jit(solution)/shard_map/all_gather | solution.py:38
  312.1 3.9 reduce_sum.18
  317.4 29.9 %all-gather.9.cloned.1.call-done = bf16[4,131072]{1,0:T(4,128)(2,1)} async-done(((bf16[4,8192]{1,0:T(4,128)(2,1)}), bf16[4,131072]{1,0:T(4,128)(2,1)}) %all-gather.9.cloned.1.call-update) | async-done | bytes 1048592 | tf_op jit(solution)/shard_map/all_gather | solution.py:58
  347.5 114.0 %while.29 = (s32[]{:T(128)}, f32[4,512,128]{2,0,1:T(4,128)S(1)}, s32[3,512]{1,0:T(4,128)S(1)}, s32[]{:T(128)}, bf16[512,128,128]{2,1,0:T(8,128)(2,1)}, /*index=5...) while((s32[]{:T(128)}, f32[4,512,128]{2,0,1:T(4,128)S(1)}, ...), condition=%wide.region_6.7_spmd, body=%wide.region_4.6_spmd.sunk | while | flops 8488966 | bytes 3023787 | solution.py:35
  347.6 1.9 gather_fusion.1
  349.5 6.5 %gather_fusion.2 = bf16[64,4,128]{2,1,0:T(4,128)(2,1)S(1)} fusion(bf16[16,4,1024,128]{3,1,2,0:T(4,128)(2,1)} %get-tuple-element.473, s32[64]{0:T(128)S(1)} %get-tuple-element.414), kind=kCustom, calls=%fused_computation.2.clone.1 | custom fusion | bytes 131584 | tf_op jit(solution)/shard_map/while/body/eval_jaxpr/gather | solution.py:65
  356.7 2.3 fusion.53
  359.0 2.7 scatter_fusion.1
  361.9 1.9 gather_fusion.1
  363.8 6.5 %gather_fusion.2 = bf16[64,4,128]{2,1,0:T(4,128)(2,1)S(1)} fusion(bf16[16,4,1024,128]{3,1,2,0:T(4,128)(2,1)} %get-tuple-element.473, s32[64]{0:T(128)S(1)} %get-tuple-element.414), kind=kCustom, calls=%fused_computation.2.clone.1 | custom fusion | bytes 131584 | tf_op jit(solution)/shard_map/while/body/eval_jaxpr/gather | solution.py:65
  371.0 2.3 fusion.53
  373.3 2.7 scatter_fusion.1
  376.1 1.9 gather_fusion.1
  378.0 6.5 %gather_fusion.2 = bf16[64,4,128]{2,1,0:T(4,128)(2,1)S(1)} fusion(bf16[16,4,1024,128]{3,1,2,0:T(4,128)(2,1)} %get-tuple-element.473, s32[64]{0:T(128)S(1)} %get-tuple-element.414), kind=kCustom, calls=%fused_computation.2.clone.1 | custom fusion | bytes 131584 | tf_op jit(solution)/shard_map/while/body/eval_jaxpr/gather | solution.py:65
  385.2 2.3 fusion.53
  387.5 2.7 scatter_fusion.1
  390.4 1.9 gather_fusion.1
  392.3 6.5 %gather_fusion.2 = bf16[64,4,128]{2,1,0:T(4,128)(2,1)S(1)} fusion(bf16[16,4,1024,128]{3,1,2,0:T(4,128)(2,1)} %get-tuple-element.473, s32[64]{0:T(128)S(1)} %get-tuple-element.414), kind=kCustom, calls=%fused_computation.2.clone.1 | custom fusion | bytes 131584 | tf_op jit(solution)/shard_map/while/body/eval_jaxpr/gather | solution.py:65
  399.5 2.3 fusion.53
  401.8 2.7 scatter_fusion.1
  404.7 1.9 gather_fusion.1
  406.5 6.5 %gather_fusion.2 = bf16[64,4,128]{2,1,0:T(4,128)(2,1)S(1)} fusion(bf16[16,4,1024,128]{3,1,2,0:T(4,128)(2,1)} %get-tuple-element.473, s32[64]{0:T(128)S(1)} %get-tuple-element.414), kind=kCustom, calls=%fused_computation.2.clone.1 | custom fusion | bytes 131584 | tf_op jit(solution)/shard_map/while/body/eval_jaxpr/gather | solution.py:65
  413.7 2.3 fusion.53
  416.0 2.7 scatter_fusion.1
  418.9 1.9 gather_fusion.1
  420.8 6.5 %gather_fusion.2 = bf16[64,4,128]{2,1,0:T(4,128)(2,1)S(1)} fusion(bf16[16,4,1024,128]{3,1,2,0:T(4,128)(2,1)} %get-tuple-element.473, s32[64]{0:T(128)S(1)} %get-tuple-element.414), kind=kCustom, calls=%fused_computation.2.clone.1 | custom fusion | bytes 131584 | tf_op jit(solution)/shard_map/while/body/eval_jaxpr/gather | solution.py:65
  428.0 2.3 fusion.53
  430.3 2.7 scatter_fusion.1
  433.2 1.9 gather_fusion.1
  435.0 6.5 %gather_fusion.2 = bf16[64,4,128]{2,1,0:T(4,128)(2,1)S(1)} fusion(bf16[16,4,1024,128]{3,1,2,0:T(4,128)(2,1)} %get-tuple-element.473, s32[64]{0:T(128)S(1)} %get-tuple-element.414), kind=kCustom, calls=%fused_computation.2.clone.1 | custom fusion | bytes 131584 | tf_op jit(solution)/shard_map/while/body/eval_jaxpr/gather | solution.py:65
  442.2 2.3 fusion.53
  444.5 2.7 scatter_fusion.1
  447.4 1.9 gather_fusion.1
  449.3 6.5 %gather_fusion.2 = bf16[64,4,128]{2,1,0:T(4,128)(2,1)S(1)} fusion(bf16[16,4,1024,128]{3,1,2,0:T(4,128)(2,1)} %get-tuple-element.473, s32[64]{0:T(128)S(1)} %get-tuple-element.414), kind=kCustom, calls=%fused_computation.2.clone.1 | custom fusion | bytes 131584 | tf_op jit(solution)/shard_map/while/body/eval_jaxpr/gather | solution.py:65
  456.5 2.3 fusion.53
  458.8 2.7 scatter_fusion.1
  462.7 108.6 %all-gather.13.cloned.1.call-done = f32[32,512,128]{2,1,0:T(8,128)} async-done(((f32[4,512,128]{2,1,0:T(8,128)}), f32[32,512,128]{2,1,0:T(8,128)}) %all-gather.13.cloned.1.call-update) | async-done | bytes 8388624 | tf_op jit(solution)/shard_map/all_gather | solution.py:38
  571.3 3.9 reduce_sum.19
  (87 shorter events, 19.8 us)
Async XLA Ops:
  6.5 309.5 %copy-start = (bf16[64,128,128]{2,1,0:T(8,128)(2,1)S(1)}, bf16[64,128,128]{2,1,0:T(8,128)(2,1)}, u32[]{:S(2)}) copy-start(bf16[64,128,128]{2,1,0:T(8,128)(2,1)} %param.15) | copy-start | bytes 6291460
  6.5 96.6 %all-gather.7.cloned.1.call-start = ((), (), s32[]{:S(2)}) async-start(), calls=%async_computation | async-start | bytes 17825792 | tf_op jit(solution)/shard_map/all_gather | solution.py:51
  7.3 304.9 %all-gather.11.cloned.1.call-start = ((), (), s32[]{:S(2)}) async-start(), calls=%async_computation.2 | async-start | bytes 9437184 | tf_op jit(solution)/shard_map/all_gather | solution.py:38
  202.8 144.6 %all-gather.9.cloned.1.call-start = ((), (), s32[]{:S(2)}) async-start(), calls=%async_computation.1 | async-start | bytes 1114112 | tf_op jit(solution)/shard_map/all_gather | solution.py:58
  317.4 253.9 %all-gather.13.cloned.1.call-start = ((), (), s32[]{:S(2)}) async-start(), calls=%async_computation.3 | async-start | bytes 9437184 | tf_op jit(solution)/shard_map/all_gather | solution.py:38
  571.3 4.6 copy-start.1
Sparse Core Ops, SparseCore 0:
  9.0 94.0 all-gather.6
  202.9 109.1 all-gather.10
  317.5 29.8 all-gather.8
  462.8 108.4 all-gather.12
